TPU v7x, 32 devices: a whole 2x2x4 slice. The times are simulated.
32 devices in a mesh: row: 4 (over y, x), col: 8 (over z, core).
Axes of the slice: x: 2, y: 2, z: 4, core: 2. Of those that a mesh axis runs over, the one named last changes fastest.
Arguments:
- noise: float32 [2048, 3072], P('row', 'col'), may hold values from -30 to 30
- images: float32 [6144, 3072], P('col', 'row'), may hold values from -6 to 6
- time_index: int32 [2048], P('row'), may hold values from 0 to 999
- w_in: float32 [3072, 3072], P(None, 'col'), may hold values from -0.109375 to 0.109375
- time_gain: float32 [3072], P('col'), may hold values from -5 to 5
- w_out: float32 [3072, 3072], P('col'), may hold values from -0.109375 to 0.109375
Outputs:
- targets: float32 [2048, 3072], P('row', 'col')
- row_pot: float32 [2048], P('row')
- col_pot: float32 [6144], P('col')
- grad_in: float32 [3072, 3072], P('row', 'col')
- grad_time: float32 [3072], P('col')
- grad_out: float32 [3072, 3072], P('col', 'row')
- mse: float32 [], replicated
All inputs are finite; a program needn't handle non-finite values.
Results may differ from a plain program's by a relative error of at most 0.0003.
Values sent between devices are 32-bit elements; how exact they have to be, the bound alone decides.
A program may use at most 128 MiB of HBM per device.

v0:
```python
import jax
import jax.numpy as jnp
from jax import lax
from jax.sharding import PartitionSpec as P

ITERS = 2
TIMES = 1000
EPSILON = 0.01


def merged(array, axis, combine):
    everything = jax.tree.map(lambda part: lax.all_gather(part, axis), array)
    first = jax.tree.map(lambda part: part[0], everything)

    def hop(k, so_far):
        return combine(so_far, jax.tree.map(lambda part: part[k], everything))

    return lax.fori_loop(1, lax.axis_size(axis), hop, first)


def joined(left_pair, right_pair):
    peak = jnp.maximum(left_pair[0], right_pair[0])
    total = left_pair[1] * jnp.exp(left_pair[0] - peak) + right_pair[1] * jnp.exp(
        right_pair[0] - peak
    )
    return (peak, total)


def over_images(logits):
    local_peak = jnp.max(logits, axis=1)
    local_total = jnp.sum(jnp.exp(logits - local_peak[:, None]), axis=1)
    peak, total = merged((local_peak, local_total), "col", joined)
    return (peak, total)


def over_noise(logits):
    local_peak = jnp.max(logits, axis=0)
    local_total = jnp.sum(jnp.exp(logits - local_peak[None, :]), axis=0)
    peak, total = merged((local_peak, local_total), "row", joined)
    return (peak, total)


def body(noise, images, time_index, w_in, time_gain, w_out):
    highest = lax.Precision.HIGHEST
    full_noise = lax.all_gather(noise, "col", axis=1, tiled=True)
    full_images = lax.all_gather(images, "row", axis=1, tiled=True)
    width = full_noise.shape[1]
    noise_count = full_noise.shape[0] * lax.axis_size("row")
    image_count = full_images.shape[0] * lax.axis_size("col")
    noise_norms = jnp.sum(full_noise * full_noise, axis=1)
    image_norms = jnp.sum(full_images * full_images, axis=1)
    cross = lax.dot_general(
        full_noise,
        full_images,
        (((1,), (1,)), ((), ())),
        precision=highest,
        preferred_element_type=jnp.float32,
    )
    scaled = (noise_norms[:, None] + image_norms[None, :] - 2.0 * cross) / (width * EPSILON)
    col_pot = jnp.zeros((full_images.shape[0],), jnp.float32)
    row_pot = jnp.zeros((full_noise.shape[0],), jnp.float32)
    for iteration in range(ITERS):
        peak, total = over_images(col_pot[None, :] - scaled)
        row_pot = jnp.log(jnp.float32(image_count)) - (jnp.log(total) + peak)
        peak, total = over_noise(row_pot[:, None] - scaled)
        col_pot = jnp.log(jnp.float32(noise_count)) - (jnp.log(total) + peak)
    logits = col_pot[None, :] - scaled
    peak, total = over_images(logits)
    weights = jnp.exp(logits - (jnp.log(total) + peak)[:, None])
    partial_value = jnp.dot(
        weights, full_images, precision=highest, preferred_element_type=jnp.float32
    )
    slice_width = noise.shape[1]
    slice_start = lax.axis_index("col") * slice_width
    whole_targets = lax.psum(partial_value, "col")
    targets = lax.dynamic_slice_in_dim(whole_targets, slice_start, slice_width, 1)
    fraction = (time_index.astype(jnp.float32) + 0.5) / TIMES
    mixed = (1.0 - fraction)[:, None] * full_noise + fraction[:, None] * whole_targets
    velocity = whole_targets - full_noise
    pre = (
        jnp.dot(mixed, w_in, precision=highest, preferred_element_type=jnp.float32)
        + fraction[:, None] * time_gain[None, :]
    )
    sigma = jax.nn.sigmoid(pre)
    hidden = pre * sigma
    part_out = jnp.dot(hidden, w_out, precision=highest, preferred_element_type=jnp.float32)
    out = lax.psum(part_out, "col")
    diff = out - velocity
    squared = jnp.sum(diff * diff)
    slope = diff / jnp.sqrt(jnp.float32(noise_count))
    local_out = lax.dot_general(
        hidden,
        slope,
        (((0,), (0,)), ((), ())),
        precision=highest,
        preferred_element_type=jnp.float32,
    )
    back = lax.dot_general(
        slope,
        w_out,
        (((1,), (1,)), ((), ())),
        precision=highest,
        preferred_element_type=jnp.float32,
    )
    dpre = back * sigma * (1.0 + pre * (1.0 - sigma))
    local_in = lax.dot_general(
        mixed, dpre, (((0,), (0,)), ((), ())), precision=highest, preferred_element_type=jnp.float32
    )
    local_time = jnp.sum(fraction[:, None] * dpre, axis=0)
    grad_in, grad_out = (
        lax.psum_scatter(local_in, "row", scatter_dimension=0, tiled=True),
        lax.psum_scatter(local_out, "row", scatter_dimension=1, tiled=True),
    )
    grad_time, squared_all = lax.psum((local_time, squared), "row")
    mse = squared_all / (noise_count * width)
    return (targets, row_pot, col_pot, grad_in, grad_time, grad_out, mse)


def solution(mesh):
    placed = (P("row", "col"), P("col", "row"), P("row"), P(None, "col"), P("col"), P("col", None))
    return jax.shard_map(
        body,
        mesh=mesh,
        in_specs=placed,
        out_specs=(
            P("row", "col"),
            P("row"),
            P("col"),
            P("row", "col"),
            P("col"),
            P("col", "row"),
            P(),
        ),
        check_vma=False,
    )
```

profile of v0, /device:TPU:0, one launch (start us, length us, event | category | flops | bytes accessed | tf_op | source)
XLA Modules:
  0.0 786.1 jit_solution(18099109052659360453)
XLA Ops:
  7.2 0.0 all-gather.23.cloned.1.call-start
  7.2 0.7 all-gather.23.cloned.1.call-update
  7.9 0.0 all-gather.25.cloned.1.call-start
  7.9 0.7 all-gather.25.cloned.1.call-update
  8.6 0.0 all-reduce.4.cloned.1.call-start
  8.7 68.3 %all-gather.23.cloned.1.call-done = f32[512,3072]{1,0:T(8,128)} async-done(((f32[512,384]{1,0:T(8,128)}), f32[512,3072]{1,0:T(8,128)}) %all-gather.23.cloned.1.call-update) | async-done | bytes 6291472 | tf_op jit(solution)/shard_map/all_gather | solution.py:45
  77.0 3.3 multiply_reduce_fusion.2
  80.3 93.5 %all-gather.25.cloned.1.call-done = f32[768,3072]{1,0:T(8,128)} async-done(((f32[768,768]{1,0:T(8,128)}), f32[768,3072]{1,0:T(8,128)}) %all-gather.25.cloned.1.call-update) | async-done | bytes 9437200 | tf_op jit(solution)/shard_map/all_gather | solution.py:46
  173.8 4.5 multiply_reduce_fusion
  178.3 1.0 copy-done
  179.2 18.3 %subtract_reduce_fusion.3 = (f32[512]{0:T(512)S(1)}, f32[512,768]{1,0:T(8,128)S(1)}) fusion(f32[512,3072]{1,0:T(8,128)S(1)} %copy-done, f32[768,3072]{1,0:T(8,128)} %all-gather.25.cloned.1.call-done, f32[768]{0:T(1024)S(1)} %multiply_reduce_fusion, f32[512]{0:T(512)S(1)} %multiply_reduce_fusion.2), kind=kOutput, calls=%fused_computation.38 | convolution fusion | flops 14497873920 | bytes 17308672 | tf_op jit(solution)/shard_map/dot_general | solution.py:52
  197.5 0.4 exponential_reduce_fusion.4
  197.9 12.8 %all-gather.11 = f32[8,1,512]{2,1,0:T(1,128)S(1)} all-gather(f32[1,1,512]{2,1,0:T(1,128)S(1)} %bitcast.95), channel_id=3, replica_groups=mesh['row'=4,'col'=8] {'col'}, dimensions={0}, use_global_device_ids=true | all-gather | bytes 18432 | tf_op jit(solution)/shard_map/all_gather | solution.py:12
  210.8 12.8 %all-gather.10 = f32[8,1,512]{2,1,0:T(1,128)S(1)} all-gather(f32[1,1,512]{2,1,0:T(1,128)S(1)} %bitcast.93), channel_id=2, replica_groups=mesh['row'=4,'col'=8] {'col'}, dimensions={0}, use_global_device_ids=true | all-gather | bytes 18432 | tf_op jit(solution)/shard_map/all_gather | solution.py:12
  223.5 0.4 while.85
  223.9 0.2 subtract_reduce_fusion.2
  224.1 0.3 exponential_reduce_fusion.3
  224.5 8.1 %all-gather.13 = f32[4,1,768]{2,1,0:T(1,128)S(1)} all-gather(f32[1,1,768]{2,1,0:T(1,128)S(1)} %reshape.65), channel_id=5, replica_groups=mesh['row'=4,'col'=8] {'row'}, dimensions={0}, use_global_device_ids=true | all-gather | bytes 15360 | tf_op jit(solution)/shard_map/all_gather | solution.py:12
  232.6 7.2 all-gather.12
  239.9 0.2 while.86
  240.1 0.2 subtract_reduce_fusion.1
  240.3 0.4 exponential_reduce_fusion.2
  240.7 12.8 %all-gather.15 = f32[8,1,512]{2,1,0:T(1,128)S(1)} all-gather(f32[1,1,512]{2,1,0:T(1,128)S(1)} %bitcast.94), channel_id=7, replica_groups=mesh['row'=4,'col'=8] {'col'}, dimensions={0}, use_global_device_ids=true | all-gather | bytes 18432 | tf_op jit(solution)/shard_map/all_gather | solution.py:12
  253.5 12.8 %all-gather.14 = f32[8,1,512]{2,1,0:T(1,128)S(1)} all-gather(f32[1,1,512]{2,1,0:T(1,128)S(1)} %bitcast.91), channel_id=6, replica_groups=mesh['row'=4,'col'=8] {'col'}, dimensions={0}, use_global_device_ids=true | all-gather | bytes 18432 | tf_op jit(solution)/shard_map/all_gather | solution.py:12
  266.3 0.4 while.87
  266.7 0.0 copy-start.5
  266.7 0.2 subtract_reduce_fusion
  266.9 0.3 exponential_reduce_fusion.1
  267.2 8.1 %all-gather.17 = f32[4,1,768]{2,1,0:T(1,128)S(1)} all-gather(f32[1,1,768]{2,1,0:T(1,128)S(1)} %reshape.73), channel_id=9, replica_groups=mesh['row'=4,'col'=8] {'row'}, dimensions={0}, use_global_device_ids=true | all-gather | bytes 15360 | tf_op jit(solution)/shard_map/all_gather | solution.py:12
  275.4 18.3 %all-gather.16 = f32[4,1,768]{2,1,0:T(1,128)S(1)} all-gather(f32[1,1,768]{2,1,0:T(1,128)S(1)} %reshape.71), channel_id=8, replica_groups=mesh['row'=4,'col'=8] {'row'}, dimensions={0}, use_global_device_ids=true | all-gather | bytes 15360 | tf_op jit(solution)/shard_map/all_gather | solution.py:12
  293.7 0.2 while.88
  293.9 0.0 copy-start.4
  293.9 0.2 subtract_reduce_fusion.4
  294.1 0.4 exponential_reduce_fusion
  294.6 12.8 %all-gather.19 = f32[8,1,512]{2,1,0:T(1,128)S(1)} all-gather(f32[1,1,512]{2,1,0:T(1,128)S(1)} %bitcast.96), channel_id=11, replica_groups=mesh['row'=4,'col'=8] {'col'}, dimensions={0}, use_global_device_ids=true | all-gather | bytes 18432 | tf_op jit(solution)/shard_map/all_gather | solution.py:12
  307.3 12.8 %all-gather.18 = f32[8,1,512]{2,1,0:T(1,128)S(1)} all-gather(f32[1,1,512]{2,1,0:T(1,128)S(1)} %bitcast.92), channel_id=10, replica_groups=mesh['row'=4,'col'=8] {'col'}, dimensions={0}, use_global_device_ids=true | all-gather | bytes 18432 | tf_op jit(solution)/shard_map/all_gather | solution.py:12
  320.1 0.4 while.89
  320.5 19.3 %fusion.6 = f32[512,3072]{1,0:T(8,128)} fusion(f32[768,3072]{1,0:T(8,128)} %all-gather.25.cloned.1.call-done, f32[512,768]{1,0:T(8,128)S(1)} %get-tuple-element.759, f32[512]{0:T(512)S(1)} %log_add_fusion, f32[768]{0:T(1024)S(1)} %add_subtract_fusion), kind=kOutput, calls=%fused_computation.26 | convolution fusion | flops 14496301056 | bytes 17306624 | tf_op jit(solution)/shard_map/dot_general | solution.py:70
  339.8 0.0 copy-start.7
  339.8 0.0 slice-start
  339.8 0.0 all-reduce.4.cloned.1.call-update
  339.8 0.0 all-reduce.6.cloned.1.call-start
  339.9 0.6 copy-done.6
  340.4 133.1 %all-reduce.4.cloned.1.call-done = f32[512,3072]{1,0:T(8,128)} async-done(((f32[512,3072]{1,0:T(8,128)}), f32[512,3072]{1,0:T(8,128)}) %all-reduce.4.cloned.1.call-update) | async-done | bytes 6291472 | tf_op jit(solution)/shard_map/psum | solution.py:75
  473.6 14.6 %convolution_add_fusion = f32[512,384]{1,0:T(8,128)S(1)} fusion(f32[3072,384]{1,0:T(8,128)} %param.19, f32[384]{0:T(512)S(1)} %copy-done.7, f32[512]{0:T(512)S(1)} %get-tuple-element.757, f32[512,3072]{1,0:T(8,128)} %all-reduce.4.cloned.1.call-done, f32[512,3072]{1,0:T(8,128)} %all-gather.23.cloned.1.call-done, f32[512]{0:T(512)S(1)} %get-tuple-element.756), kind=kOutput, calls=%fused_computation.43 | convolution fusion | flops 7252869120 | bytes 18093568 | tf_op jit(solution)/shard_map/dot_general | solution.py:81
  488.2 0.0 copy-start.2
  488.2 0.9 copy-done.2
  489.1 12.0 %fusion.20 = f32[512,3072]{1,0:T(8,128)} fusion(f32[384,3072]{1,0:T(8,128)S(1)} %bitcast.68, f32[512,384]{1,0:T(8,128)S(1)} %convolution_add_fusion), kind=kOutput, calls=%fused_computation.49 | convolution fusion | flops 7248543744 | bytes 11796480 | tf_op jit(solution)/shard_map/dot_general | solution.py:86
  501.1 0.0 all-reduce.6.cloned.1.call-update
  501.1 0.3 reduce-scatter.5.cloned.1.call-start
  501.4 136.0 %all-reduce.6.cloned.1.call-done = f32[512,3072]{1,0:T(8,128)} async-done(((f32[512,3072]{1,0:T(8,128)}), f32[512,3072]{1,0:T(8,128)}) %all-reduce.6.cloned.1.call-update) | async-done | bytes 6291472 | tf_op jit(solution)/shard_map/psum | solution.py:87
  637.3 9.5 %multiply_reduce_fusion.1 = (f32[]{:T(128)}, f32[512,3072]{1,0:T(8,128)S(1)}) fusion(f32[512,3072]{1,0:T(8,128)} %all-reduce.6.cloned.1.call-done, f32[512,3072]{1,0:T(8,128)} %all-reduce.4.cloned.1.call-done, f32[512,3072]{1,0:T(8,128)} %all-gather.23.cloned.1.call-done), kind=kLoop, calls=%fused_computation.16 | loop fusion | flops 6291455 | bytes 25165828 | tf_op jit(solution)/shard_map/reduce_sum | solution.py:89
  646.8 2.6 copy-done.1
  649.4 10.6 %fusion = f32[384,3072]{1,0:T(8,128)} fusion(f32[512,3072]{1,0:T(8,128)S(1)} %get-tuple-element.745, f32[512,384]{1,0:T(8,128)} %copy-done.2), kind=kOutput, calls=%fused_computation.20 | convolution fusion | flops 7250116608 | bytes 11796480 | tf_op jit(solution)/shard_map/dot_general | solution.py:91
  660.1 0.0 reduce-scatter.5.cloned.1.call-update
  660.1 0.3 reduce-scatter.3.cloned.1.call-start
  660.4 0.8 copy-done.3
  661.2 14.1 %multiply_reduce_fusion.3 = (f32[384]{0:T(512)S(1)}, f32[512,384]{1,0:T(8,128)S(1)}) fusion(f32[512]{0:T(512)S(1)} %get-tuple-element.757, f32[512,384]{1,0:T(8,128)S(1)} %copy-done.3, f32[384,3072]{1,0:T(8,128)} %param.21, f32[512,3072]{1,0:T(8,128)} %copy-done.1), kind=kOutput, calls=%fused_computation.44 | convolution fusion | flops 7251295744 | bytes 12586496 | tf_op jit(solution)/shard_map/dot_general | solution.py:98
  675.3 15.4 %fusion.26 = f32[3072,384]{1,0:T(8,128)} fusion(f32[512,384]{1,0:T(8,128)S(1)} %get-tuple-element.761, f32[512,3072]{1,0:T(8,128)} %all-reduce.4.cloned.1.call-done, f32[512,3072]{1,0:T(8,128)} %all-gather.23.cloned.1.call-done, f32[512]{0:T(512)S(1)} %get-tuple-element.757, f32[512]{0:T(512)S(1)} %get-tuple-element.756), kind=kOutput, calls=%fused_computation.76 | convolution fusion | flops 7252475904 | bytes 18092032 | tf_op jit(solution)/shard_map/dot_general | solution.py:106
  690.7 0.0 reduce-scatter.3.cloned.1.call-update
  690.7 2.1 constant_dynamic-slice_fusion.6
  692.8 10.5 %all-reduce = (f32[384]{0:T(512)}, f32[]{:T(128)}) all-reduce(f32[384]{0:T(512)S(1)} %get-tuple-element.760, f32[]{:T(128)} %get-tuple-element.744), channel_id=1, replica_groups=mesh['row'=4,'col'=8] {'row'}, use_global_device_ids=true, to_apply=%region_26.0 | all-reduce | flops 385 | bytes 3080 | tf_op jit(solution)/shard_map/psum | solution.py:114
  703.9 13.4 %reduce-scatter.5.cloned.1.call-done = f32[384,768]{1,0:T(8,128)} async-done(((f32[384,3072]{1,0:T(8,128)}), f32[384,768]{1,0:T(8,128)}) %reduce-scatter.5.cloned.1.call-update) | async-done | bytes 1179664 | tf_op jit(solution)/shard_map/reduce_scatter | solution.py:112
  717.3 60.4 %reduce-scatter.3.cloned.1.call-done = f32[768,384]{1,0:T(8,128)} async-done(((f32[3072,384]{1,0:T(8,128)}), f32[768,384]{1,0:T(8,128)}) %reduce-scatter.3.cloned.1.call-update) | async-done | bytes 1179664 | tf_op jit(solution)/shard_map/reduce_scatter | solution.py:111
  (95 shorter events, 1.0 us)
Async XLA Ops:
  7.2 69.9 %all-gather.23.cloned.1.call-start = ((), (), s32[]{:S(2)}) async-start(), calls=%async_computation.2 | async-start | bytes 7077888 | tf_op jit(solution)/shard_map/all_gather | solution.py:45
  7.9 165.9 %all-gather.25.cloned.1.call-start = ((), (), s32[]{:S(2)}) async-start(), calls=%async_computation.3 | async-start | bytes 11796480 | tf_op jit(solution)/shard_map/all_gather | solution.py:46
  8.6 464.9 %all-reduce.4.cloned.1.call-start = ((), (), s32[]{:S(2)}) async-start(), calls=%async_computation.4 | async-start | bytes 12582912 | tf_op jit(solution)/shard_map/psum | solution.py:75
  173.8 5.5 copy-start
  266.7 73.1 %copy-start.5 = (f32[512]{0:T(512)}, f32[512]{0:T(512)S(1)}, u32[]{:S(2)}) copy-start(f32[512]{0:T(512)S(1)} %add_subtract_fusion.2) | copy-start | bytes 6148
  293.9 45.8 %copy-start.4 = (f32[768]{0:T(1024)}, f32[768]{0:T(1024)S(1)}, u32[]{:S(2)}) copy-start(f32[768]{0:T(1024)S(1)} %add_subtract_fusion) | copy-start | bytes 9220
  339.8 0.7 copy-start.6
  339.8 133.8 %copy-start.7 = (f32[384]{0:T(512)S(1)}, f32[384]{0:T(512)}, u32[]{:S(2)}) copy-start(f32[384]{0:T(512)} %param.20) | copy-start | bytes 4612
  339.8 149.3 %slice-start = ((s8[4718592]{0:T(1024)(128)(4,1)}), s8[524288]{0:T(1024)(128)(4,1)S(1)}, s32[]{:S(2)}) async-start(s8[4718592]{0:T(1024)(128)(4,1)} %bitcast.67), calls=%async_computation.8 | async-start | bytes 1048576
  339.8 297.5 %all-reduce.6.cloned.1.call-start = ((), (), s32[]{:S(2)}) async-start(), calls=%async_computation.5 | async-start | bytes 12582912 | tf_op jit(solution)/shard_map/psum | solution.py:87
  473.6 15.5 %slice-start.1 = ((s8[4718592]{0:T(1024)(128)(4,1)}), s8[4194304]{0:T(1024)(128)(4,1)S(1)}, s32[]{:S(2)}) async-start(s8[4718592]{0:T(1024)(128)(4,1)} %bitcast.67), calls=%async_computation.9 | async-start | bytes 8388608
  488.2 0.9 copy-start.2
  501.1 216.2 %reduce-scatter.5.cloned.1.call-start = ((), (), s32[]{:S(2)}) async-start(), calls=%async_computation.7 | async-start | bytes 5898240 | tf_op jit(solution)/shard_map/reduce_scatter | solution.py:112
  646.8 2.6 copy-start.1
  660.1 1.1 copy-start.3
  660.1 117.6 %reduce-scatter.3.cloned.1.call-start = ((), (), s32[]{:S(2)}) async-start(), calls=%async_computation.6 | async-start | bytes 5898240 | tf_op jit(solution)/shard_map/reduce_scatter | solution.py:111
Sparse Core Ops, SparseCore 0:
  9.6 67.4 all-gather.22
  78.9 94.8 all-gather.24
  339.9 133.6 all-reduce.3
  501.2 136.0 all-reduce.5
  660.2 57.0 reduce-scatter.4
  720.7 56.9 reduce-scatter.2
where the time goes:
time: 794 us; the launch traced here: 786 us
  waiting for transfers between devices  506 us (64%)
  blocking collectives  129 us (16%)
  matrix products  104 us (13%)
  other arithmetic  20.5 us (3%)
  between operations  16.6 us (2%)
  local copies, waits for them, and re-layouts  8.41 us (1%)
    psum x1, waiting for transfers between devices, body(): out = lax.psum(part_out, 'col')  136 us
    psum x1, waiting for transfers between devices, body(): whole_targets = lax.psum(partial_value, 'col')  133 us
    all_gather x10, blocking collectives, merged(): everything = jax.tree.map(lambda part: lax.all_gather(part, axis), array)  118 us
    all_gather x1, waiting for transfers between devices, body(): full_images = lax.all_gather(images, 'row', axis=1, tiled=True)  93.5 us
    all_gather x1, waiting for transfers between devices, body(): full_noise = lax.all_gather(noise, 'col', axis=1, tiled=True)  68.3 us
    reduce_scatter x1, waiting for transfers between devices, body(): lax.psum_scatter(local_in, 'row', scatter_dimension=0, tiled=True)  60.4 us
    dot_general x1, matrix products, body(): jnp.dot(weights, full_images, precision=highest, preferred_element_type=j...  19.3 us
    dot_general x1, matrix products, body(): lax.dot_general(full_noise, full_images, (((1,), (1,)), ((), ())), precis...  18.3 us
  transfers between devices with their start and end apart: 6, of which 6 were waited for; matrix products, arithmetic and copies ran while one was open for 4% of the time, Pallas kernels for 0%

commit v1 on v0

--- a/solution.py
+++ b/solution.py
@@ -6,6 +6,16 @@
 ITERS = 2
 TIMES = 1000
 EPSILON = 0.01
+
+
+def gather_by_hops(block, axis, along):
+    n_dev = lax.axis_size(axis)
+    moving, blocks = (block, [block])
+    for _ in range(n_dev - 1):
+        moving = lax.ppermute(moving, axis, [(i, (i + 1) % n_dev) for i in range(n_dev)])
+        blocks.insert(0, moving)
+    line = jnp.concatenate(blocks, axis=along)
+    return jnp.roll(line, (lax.axis_index(axis) + 1) * block.shape[along], axis=along)
 
 
 def merged(array, axis, combine):
@@ -42,7 +52,7 @@
 
 def body(noise, images, time_index, w_in, time_gain, w_out):
     highest = lax.Precision.HIGHEST
-    full_noise = lax.all_gather(noise, "col", axis=1, tiled=True)
+    full_noise = gather_by_hops(noise, "col", 1)
     full_images = lax.all_gather(images, "row", axis=1, tiled=True)
     width = full_noise.shape[1]
     noise_count = full_noise.shape[0] * lax.axis_size("row")

time: 794 us -> 728 us (0.917)
  waiting for transfers between devices: 506 us -> 436 us
  local copies, waits for them, and re-layouts: 8.41 us -> 19.8 us
  blocking collectives: 129 us -> 120 us
    ppermute x0 -> x7, waiting for transfers between devices: none -> 93.6 us  [gather_by_hops(): lax.ppermute(moving, axis, [(i, (i + 1) % n_dev) for i in range(n_dev)])]
    all_gather x1, waiting for transfers between devices: 93.5 us -> 0.02 us  [body(): full_images = lax.all_gather(images, 'row', axis=1, tiled=True)]
    all_gather x1 -> x0, waiting for transfers between devices: 68.3 us -> none  [body(): full_noise = lax.all_gather(noise, 'col', axis=1, tiled=True)]
    unnamed x34 -> x55, local copies, waits for them, and re-layouts: 5.92 us -> 17.2 us
    all_gather x10, blocking collectives: 118 us -> 109 us  [merged(): everything = jax.tree.map(lambda part: lax.all_gather(part, axis), array)]
  transfers between devices with their start and end apart: 6 -> 12, of which waited for: 6 -> 11; matrix products, arithmetic and copies ran while one was open for 4% -> 6% of each run, Pallas kernels for 0% -> 0%
where the time goes in v1:
time: 728 us; the launch traced here: 724 us
  waiting for transfers between devices  436 us (60%)
  blocking collectives  120 us (16%)
  matrix products  108 us (15%)
  other arithmetic  21.8 us (3%)
  local copies, waits for them, and re-layouts  19.8 us (3%)
  between operations  16.5 us (2%)
    psum x1, waiting for transfers between devices, body(): out = lax.psum(part_out, 'col')  136 us
    psum x1, waiting for transfers between devices, body(): whole_targets = lax.psum(partial_value, 'col')  133 us
    all_gather x10, blocking collectives, merged(): everything = jax.tree.map(lambda part: lax.all_gather(part, axis), array)  109 us
    ppermute x7, waiting for transfers between devices, gather_by_hops(): lax.ppermute(moving, axis, [(i, (i + 1) % n_dev) for i in range(n_dev)])  93.6 us
    reduce_scatter x1, waiting for transfers between devices, body(): lax.psum_scatter(local_in, 'row', scatter_dimension=0, tiled=True)  60.3 us
    dot_general x1, matrix products, body(): jnp.dot(weights, full_images, precision=highest, preferred_element_type=j...  19.3 us
    dot_general x1, matrix products, body(): lax.dot_general(full_noise, full_images, (((1,), (1,)), ((), ())), precis...  18.9 us
    dot_general x1, matrix products, body(): lax.dot_general(mixed, dpre, (((0,), (0,)), ((), ())), precision=highest,...  17.4 us
  transfers between devices with their start and end apart: 12, of which 11 were waited for; matrix products, arithmetic and copies ran while one was open for 6% of the time, Pallas kernels for 0%

profile of v1, /device:TPU:0, one launch (start us, length us, event | category | flops | bytes accessed | tf_op | source)
XLA Modules:
  0.0 723.7 jit_solution(12935812223855508904)
XLA Ops:
  7.2 0.7 all-gather.22.cloned.1.call-update
  8.0 0.5 collective-permute-start
  8.5 13.9 %collective-permute-done = f32[512,384]{1,0:T(8,128)S(1)} collective-permute-done((f32[512,384]{1,0:T(8,128)}, f32[512,384]{1,0:T(8,128)S(1)}, u32[]{:S(2)}, u32[]{:S(2)}) %collective-permute-start) | collective-permute-done | bytes 786464 | tf_op jit(solution)/shard_map/ppermute | solution.py:15
  22.4 13.2 %collective-permute-done.1 = f32[512,384]{1,0:T(8,128)S(1)} collective-permute-done((f32[512,384]{1,0:T(8,128)S(1)}, f32[512,384]{1,0:T(8,128)S(1)}, u32[]{:S(2)}, u32[]{:S(2)}) %collective-permute-start.1) | collective-permute-done | bytes 786464 | tf_op jit(solution)/shard_map/ppermute | solution.py:15
  35.6 13.2 %collective-permute-done.2 = f32[512,384]{1,0:T(8,128)S(1)} collective-permute-done((f32[512,384]{1,0:T(8,128)S(1)}, f32[512,384]{1,0:T(8,128)S(1)}, u32[]{:S(2)}, u32[]{:S(2)}) %collective-permute-start.2) | collective-permute-done | bytes 786464 | tf_op jit(solution)/shard_map/ppermute | solution.py:15
  48.8 13.2 %collective-permute-done.3 = f32[512,384]{1,0:T(8,128)S(1)} collective-permute-done((f32[512,384]{1,0:T(8,128)S(1)}, f32[512,384]{1,0:T(8,128)S(1)}, u32[]{:S(2)}, u32[]{:S(2)}) %collective-permute-start.3) | collective-permute-done | bytes 786464 | tf_op jit(solution)/shard_map/ppermute | solution.py:15
  62.1 0.9 copy-done.3
  62.9 13.2 %collective-permute-done.4 = f32[512,384]{1,0:T(8,128)S(1)} collective-permute-done((f32[512,384]{1,0:T(8,128)S(1)}, f32[512,384]{1,0:T(8,128)S(1)}, u32[]{:S(2)}, u32[]{:S(2)}) %collective-permute-start.4) | collective-permute-done | bytes 786464 | tf_op jit(solution)/shard_map/ppermute | solution.py:15
  76.1 0.9 copy-done.5
  77.0 13.3 %collective-permute-done.5 = f32[512,384]{1,0:T(8,128)} collective-permute-done((f32[512,384]{1,0:T(8,128)S(1)}, f32[512,384]{1,0:T(8,128)}, u32[]{:S(2)}, u32[]{:S(2)}) %collective-permute-start.5) | collective-permute-done | bytes 786464 | tf_op jit(solution)/shard_map/ppermute | solution.py:15
  90.3 13.5 %collective-permute-done.6 = f32[512,384]{1,0:T(8,128)} collective-permute-done((f32[512,384]{1,0:T(8,128)}, f32[512,384]{1,0:T(8,128)}, u32[]{:S(2)}, u32[]{:S(2)}) %collective-permute-start.6) | collective-permute-done | bytes 786464 | tf_op jit(solution)/shard_map/ppermute | solution.py:15
  103.9 1.2 constant_dynamic-update-slice_fusion.15
  105.1 1.2 constant_dynamic-update-slice_fusion.14
  106.4 1.3 constant_dynamic-update-slice_fusion.13
  107.7 1.3 constant_dynamic-update-slice_fusion.12
  109.2 0.1 constant_dynamic-update-slice_fusion.9
  109.4 1.2 constant_dynamic-update-slice_fusion.7
  110.6 1.2 constant_dynamic-update-slice_fusion.6
  112.1 0.1 constant_dynamic-update-slice_fusion.3
  112.3 0.1 constant_dynamic-update-slice_fusion.1
  112.5 4.6 copy-done
  117.1 1.9 multiply_reduce_fusion.2
  119.1 4.5 multiply_reduce_fusion
  123.6 1.8 copy-done.1
  125.4 18.9 %subtract_reduce_fusion.3 = (f32[512]{0:T(512)S(1)}, f32[512,768]{1,0:T(8,128)S(1)}) fusion(f32[768,3072]{1,0:T(8,128)S(1)} %copy-done.1, f32[512,6144]{1,0:T(8,128)} %copy-done, s32[]{:T(128)S(6)} %select_n.72, f32[768]{0:T(1024)S(1)} %multiply_reduce_fusion, f32[512]{0:T(512)S(1)} %multiply_reduce_fusion.2), kind=kOutput, calls=%fused_computation.40 | convolution fusion | flops 14497873920 | bytes 17308676 | tf_op jit(solution)/shard_map/dot_general | solution.py:62
  144.3 0.4 exponential_reduce_fusion.4
  144.7 12.8 %all-gather.11 = f32[8,1,512]{2,1,0:T(1,128)S(1)} all-gather(f32[1,1,512]{2,1,0:T(1,128)S(1)} %bitcast.94), channel_id=3, replica_groups=mesh['row'=4,'col'=8] {'col'}, dimensions={0}, use_global_device_ids=true | all-gather | bytes 18432 | tf_op jit(solution)/shard_map/all_gather | solution.py:22
  157.5 12.8 %all-gather.10 = f32[8,1,512]{2,1,0:T(1,128)S(1)} all-gather(f32[1,1,512]{2,1,0:T(1,128)S(1)} %bitcast.92), channel_id=2, replica_groups=mesh['row'=4,'col'=8] {'col'}, dimensions={0}, use_global_device_ids=true | all-gather | bytes 18432 | tf_op jit(solution)/shard_map/all_gather | solution.py:22
  170.3 0.4 while.85
  170.7 0.2 subtract_reduce_fusion.2
  170.9 0.3 exponential_reduce_fusion.3
  171.2 8.7 %all-gather.13 = f32[4,1,768]{2,1,0:T(1,128)S(1)} all-gather(f32[1,1,768]{2,1,0:T(1,128)S(1)} %reshape.65), channel_id=5, replica_groups=mesh['row'=4,'col'=8] {'row'}, dimensions={0}, use_global_device_ids=true | all-gather | bytes 15360 | tf_op jit(solution)/shard_map/all_gather | solution.py:22
  179.9 8.1 %all-gather.12 = f32[4,1,768]{2,1,0:T(1,128)S(1)} all-gather(f32[1,1,768]{2,1,0:T(1,128)S(1)} %reshape.63), channel_id=4, replica_groups=mesh['row'=4,'col'=8] {'row'}, dimensions={0}, use_global_device_ids=true | all-gather | bytes 15360 | tf_op jit(solution)/shard_map/all_gather | solution.py:22
  188.1 0.2 while.86
  188.3 0.2 subtract_reduce_fusion.1
  188.5 0.4 exponential_reduce_fusion.2
  188.9 12.8 %all-gather.15 = f32[8,1,512]{2,1,0:T(1,128)S(1)} all-gather(f32[1,1,512]{2,1,0:T(1,128)S(1)} %bitcast.93), channel_id=7, replica_groups=mesh['row'=4,'col'=8] {'col'}, dimensions={0}, use_global_device_ids=true | all-gather | bytes 18432 | tf_op jit(solution)/shard_map/all_gather | solution.py:22
  201.7 12.8 %all-gather.14 = f32[8,1,512]{2,1,0:T(1,128)S(1)} all-gather(f32[1,1,512]{2,1,0:T(1,128)S(1)} %bitcast.90), channel_id=6, replica_groups=mesh['row'=4,'col'=8] {'col'}, dimensions={0}, use_global_device_ids=true | all-gather | bytes 18432 | tf_op jit(solution)/shard_map/all_gather | solution.py:22
  214.5 0.5 while.87
  215.1 0.2 subtract_reduce_fusion
  215.3 0.3 exponential_reduce_fusion.1
  215.6 7.2 all-gather.17
  222.8 8.1 %all-gather.16 = f32[4,1,768]{2,1,0:T(1,128)S(1)} all-gather(f32[1,1,768]{2,1,0:T(1,128)S(1)} %reshape.71), channel_id=8, replica_groups=mesh['row'=4,'col'=8] {'row'}, dimensions={0}, use_global_device_ids=true | all-gather | bytes 15360 | tf_op jit(solution)/shard_map/all_gather | solution.py:22
  231.0 0.2 while.88
  231.3 0.2 subtract_reduce_fusion.4
  231.4 0.4 exponential_reduce_fusion
  231.9 12.8 %all-gather.19 = f32[8,1,512]{2,1,0:T(1,128)S(1)} all-gather(f32[1,1,512]{2,1,0:T(1,128)S(1)} %bitcast.95), channel_id=11, replica_groups=mesh['row'=4,'col'=8] {'col'}, dimensions={0}, use_global_device_ids=true | all-gather | bytes 18432 | tf_op jit(solution)/shard_map/all_gather | solution.py:22
  244.7 12.8 %all-gather.18 = f32[8,1,512]{2,1,0:T(1,128)S(1)} all-gather(f32[1,1,512]{2,1,0:T(1,128)S(1)} %bitcast.91), channel_id=10, replica_groups=mesh['row'=4,'col'=8] {'col'}, dimensions={0}, use_global_device_ids=true | all-gather | bytes 18432 | tf_op jit(solution)/shard_map/all_gather | solution.py:22
  257.4 0.4 while.89
  257.8 19.3 %fusion.8 = f32[512,3072]{1,0:T(8,128)} fusion(f32[768,3072]{1,0:T(8,128)} %all-gather.22.cloned.1.call-done, f32[512,768]{1,0:T(8,128)S(1)} %get-tuple-element.759, f32[512]{0:T(512)S(1)} %log_add_fusion, f32[768]{0:T(1024)S(1)} %add_subtract_fusion), kind=kOutput, calls=%fused_computation.28 | convolution fusion | flops 14496301056 | bytes 17306624 | tf_op jit(solution)/shard_map/dot_general | solution.py:80
  277.2 0.6 copy-done.10
  277.8 133.1 %all-reduce.4.cloned.1.call-done = f32[512,3072]{1,0:T(8,128)} async-done(((f32[512,3072]{1,0:T(8,128)}), f32[512,3072]{1,0:T(8,128)}) %all-reduce.4.cloned.1.call-update) | async-done | bytes 6291472 | tf_op jit(solution)/shard_map/psum | solution.py:85
  411.0 15.1 %convolution_add_fusion = f32[512,384]{1,0:T(8,128)S(1)} fusion(f32[3072,384]{1,0:T(8,128)} %param.19, f32[384]{0:T(512)S(1)} %copy-done.9, f32[512]{0:T(512)S(1)} %get-tuple-element.757, f32[512,3072]{1,0:T(8,128)} %all-reduce.4.cloned.1.call-done, f32[512,6144]{1,0:T(8,128)} %copy-done, s32[]{:T(128)S(6)} %select_n.72, f32[512]{0:T(512)S(1)} %get-tuple-element.756), kind=kOutput, calls=%fused_computation.45 | convolution fusion | flops 7252869120 | bytes 18096132 | tf_op jit(solution)/shard_map/dot_general | solution.py:91
  426.1 12.1 %fusion.24 = f32[512,3072]{1,0:T(8,128)} fusion(f32[384,3072]{1,0:T(8,128)S(1)} %bitcast.67, f32[512,384]{1,0:T(8,128)S(1)} %convolution_add_fusion), kind=kOutput, calls=%fused_computation.51 | convolution fusion | flops 7248543744 | bytes 11796480 | tf_op jit(solution)/shard_map/dot_general | solution.py:96
  438.2 0.3 reduce-scatter.5.cloned.1.call-start
  438.5 135.9 %all-reduce.6.cloned.1.call-done = f32[512,3072]{1,0:T(8,128)} async-done(((f32[512,3072]{1,0:T(8,128)}), f32[512,3072]{1,0:T(8,128)}) %all-reduce.6.cloned.1.call-update) | async-done | bytes 6291472 | tf_op jit(solution)/shard_map/psum | solution.py:97
  574.5 12.2 %multiply_reduce_fusion.1 = (f32[]{:T(128)}, f32[512,3072]{1,0:T(8,128)}) fusion(f32[512,3072]{1,0:T(8,128)} %all-reduce.6.cloned.1.call-done, f32[512,3072]{1,0:T(8,128)} %all-reduce.4.cloned.1.call-done, f32[512,6144]{1,0:T(8,128)} %copy-done, s32[]{:T(128)S(6)} %select_n.72), kind=kLoop, calls=%fused_computation.16 | loop fusion | flops 6291455 | bytes 25165832 | tf_op jit(solution)/shard_map/reduce_sum | solution.py:99
  586.6 11.4 %fusion = f32[384,3072]{1,0:T(8,128)} fusion(f32[512,3072]{1,0:T(8,128)} %get-tuple-element.745, f32[512,384]{1,0:T(8,128)S(1)} %convolution_add_fusion), kind=kOutput, calls=%fused_computation.20 | convolution fusion | flops 7250116608 | bytes 11796480 | tf_op jit(solution)/shard_map/dot_general | solution.py:101
  598.1 14.1 %multiply_reduce_fusion.3 = (f32[384]{0:T(512)S(1)}, f32[512,384]{1,0:T(8,128)S(1)}) fusion(f32[512]{0:T(512)S(1)} %get-tuple-element.757, f32[512,384]{1,0:T(8,128)S(1)} %convolution_add_fusion, f32[384,3072]{1,0:T(8,128)} %param.21, f32[512,3072]{1,0:T(8,128)} %get-tuple-element.745), kind=kOutput, calls=%fused_computation.46 | convolution fusion | flops 7251295744 | bytes 12586496 | tf_op jit(solution)/shard_map/dot_general | solution.py:108
  612.1 17.4 %fusion.31 = f32[3072,384]{1,0:T(8,128)} fusion(f32[512,384]{1,0:T(8,128)S(1)} %get-tuple-element.761, f32[512,3072]{1,0:T(8,128)} %all-reduce.4.cloned.1.call-done, f32[512,6144]{1,0:T(8,128)} %copy-done, s32[]{:T(128)S(6)} %select_n.72, f32[512]{0:T(512)S(1)} %get-tuple-element.757, f32[512]{0:T(512)S(1)} %get-tuple-element.756), kind=kOutput, calls=%fused_computation.95 | convolution fusion | flops 7252475904 | bytes 18092036 | tf_op jit(solution)/shard_map/dot_general | solution.py:116
  629.6 2.1 constant_dynamic-slice_fusion.6
  631.7 10.9 %all-reduce = (f32[384]{0:T(512)}, f32[]{:T(128)}) all-reduce(f32[384]{0:T(512)S(1)} %get-tuple-element.760, f32[]{:T(128)} %get-tuple-element.744), channel_id=1, replica_groups=mesh['row'=4,'col'=8] {'row'}, use_global_device_ids=true, to_apply=%region_26.27 | all-reduce | flops 385 | bytes 3080 | tf_op jit(solution)/shard_map/psum | solution.py:124
  643.2 12.0 %reduce-scatter.5.cloned.1.call-done = f32[384,768]{1,0:T(8,128)} async-done(((f32[384,3072]{1,0:T(8,128)}), f32[384,768]{1,0:T(8,128)}) %reduce-scatter.5.cloned.1.call-update) | async-done | bytes 1179664 | tf_op jit(solution)/shard_map/reduce_scatter | solution.py:122
  655.3 60.3 %reduce-scatter.3.cloned.1.call-done = f32[768,384]{1,0:T(8,128)} async-done(((f32[3072,384]{1,0:T(8,128)}), f32[768,384]{1,0:T(8,128)}) %reduce-scatter.3.cloned.1.call-update) | async-done | bytes 1179664 | tf_op jit(solution)/shard_map/reduce_scatter | solution.py:121
  (128 shorter events, 2.0 us)
Async XLA Ops:
  7.2 102.1 %copy-start.2 = (f32[512,384]{1,0:T(8,128)S(1)}, f32[512,384]{1,0:T(8,128)}, u32[]{:S(2)}) copy-start(f32[512,384]{1,0:T(8,128)} %param.16) | copy-start | bytes 2359300
  7.2 111.9 %all-gather.22.cloned.1.call-start = ((), (), s32[]{:S(2)}) async-start(), calls=%async_computation.2 | async-start | bytes 11796480 | tf_op jit(solution)/shard_map/all_gather | solution.py:56
  7.9 403.0 %all-reduce.4.cloned.1.call-start = ((), (), s32[]{:S(2)}) async-start(), calls=%async_computation.3 | async-start | bytes 12582912 | tf_op jit(solution)/shard_map/psum | solution.py:85
  8.0 14.5 %collective-permute-start = (f32[512,384]{1,0:T(8,128)}, f32[512,384]{1,0:T(8,128)S(1)}, u32[]{:S(2)}, u32[]{:S(2)}) collective-permute-start(f32[512,384]{1,0:T(8,128)} %param.16), channel_id=1, source_target_pairs={{0,1},{1,2},{2,3},{3,4},{4,5},{5,6},{6,7},{7,0},{8,9},{9,10},{10,1... | collective-permute-start | bytes 2359304 | tf_op jit(solution)/shard_map/ppermute | solution.py:15
  22.4 13.2 %collective-permute-start.1 = (f32[512,384]{1,0:T(8,128)S(1)}, f32[512,384]{1,0:T(8,128)S(1)}, u32[]{:S(2)}, u32[]{:S(2)}) collective-permute-start(f32[512,384]{1,0:T(8,128)S(1)} %collective-permute-done), channel_id=1, source_target_pairs={{0,1},{1,2},{2,3},{3,4},{4,5},{5,6},{6,7},{7,0},{8,9},{9,10},{10,1... | collective-permute-start | bytes 2359304 | tf_op jit(solution)/shard_map/ppermute | solution.py:15
  35.6 13.2 %collective-permute-start.2 = (f32[512,384]{1,0:T(8,128)S(1)}, f32[512,384]{1,0:T(8,128)S(1)}, u32[]{:S(2)}, u32[]{:S(2)}) collective-permute-start(f32[512,384]{1,0:T(8,128)S(1)} %collective-permute-done.1), channel_id=1, source_target_pairs={{0,1},{1,2},{2,3},{3,4},{4,5},{5,6},{6,7},{7,0},{8,9},{9,10},{10,1... | collective-permute-start | bytes 2359304 | tf_op jit(solution)/shard_map/ppermute | solution.py:15
  48.8 13.2 %collective-permute-start.3 = (f32[512,384]{1,0:T(8,128)S(1)}, f32[512,384]{1,0:T(8,128)S(1)}, u32[]{:S(2)}, u32[]{:S(2)}) collective-permute-start(f32[512,384]{1,0:T(8,128)S(1)} %collective-permute-done.2), channel_id=1, source_target_pairs={{0,1},{1,2},{2,3},{3,4},{4,5},{5,6},{6,7},{7,0},{8,9},{9,10},{10,1... | collective-permute-start | bytes 2359304 | tf_op jit(solution)/shard_map/ppermute | solution.py:15
  62.1 0.9 copy-start.3
  62.9 13.2 %collective-permute-start.4 = (f32[512,384]{1,0:T(8,128)S(1)}, f32[512,384]{1,0:T(8,128)S(1)}, u32[]{:S(2)}, u32[]{:S(2)}) collective-permute-start(f32[512,384]{1,0:T(8,128)S(1)} %collective-permute-done.3), channel_id=1, source_target_pairs={{0,1},{1,2},{2,3},{3,4},{4,5},{5,6},{6,7},{7,0},{8,9},{9,10},{10,1... | collective-permute-start | bytes 2359304 | tf_op jit(solution)/shard_map/ppermute | solution.py:15
  76.1 0.9 copy-start.5
  77.0 13.3 %collective-permute-start.5 = (f32[512,384]{1,0:T(8,128)S(1)}, f32[512,384]{1,0:T(8,128)}, u32[]{:S(2)}, u32[]{:S(2)}) collective-permute-start(f32[512,384]{1,0:T(8,128)S(1)} %collective-permute-done.4), channel_id=1, source_target_pairs={{0,1},{1,2},{2,3},{3,4},{4,5},{5,6},{6,7},{7,0},{8,9},{9,10},{10,1... | collective-permute-start | bytes 2359304 | tf_op jit(solution)/shard_map/ppermute | solution.py:15
  90.3 13.5 %collective-permute-start.6 = (f32[512,384]{1,0:T(8,128)}, f32[512,384]{1,0:T(8,128)}, u32[]{:S(2)}, u32[]{:S(2)}) collective-permute-start(f32[512,384]{1,0:T(8,128)} %collective-permute-done.5), channel_id=1, source_target_pairs={{0,1},{1,2},{2,3},{3,4},{4,5},{5,6},{6,7},{7,0},{8,9},{9,10},{10,1... | collective-permute-start | bytes 2359304 | tf_op jit(solution)/shard_map/ppermute | solution.py:15
  106.3 5.5 copy-start.6
  107.7 4.3 copy-start.4
  112.5 4.6 copy-start
  119.0 6.4 copy-start.1
  215.1 62.1 %copy-start.8 = (f32[512]{0:T(512)}, f32[512]{0:T(512)S(1)}, u32[]{:S(2)}) copy-start(f32[512]{0:T(512)S(1)} %add_subtract_fusion.2) | copy-start | bytes 6148
  231.2 45.9 %copy-start.7 = (f32[768]{0:T(1024)}, f32[768]{0:T(1024)S(1)}, u32[]{:S(2)}) copy-start(f32[768]{0:T(1024)S(1)} %add_subtract_fusion) | copy-start | bytes 9220
  277.1 0.7 copy-start.10
  277.1 133.8 %copy-start.9 = (f32[384]{0:T(512)S(1)}, f32[384]{0:T(512)}, u32[]{:S(2)}) copy-start(f32[384]{0:T(512)} %param.20) | copy-start | bytes 4612
  277.1 149.0 %slice-start = ((s8[4718592]{0:T(1024)(128)(4,1)}), s8[524288]{0:T(1024)(128)(4,1)S(1)}, s32[]{:S(2)}) async-start(s8[4718592]{0:T(1024)(128)(4,1)} %bitcast.66), calls=%async_computation.7 | async-start | bytes 1048576
  277.2 297.3 %all-reduce.6.cloned.1.call-start = ((), (), s32[]{:S(2)}) async-start(), calls=%async_computation.4 | async-start | bytes 12582912 | tf_op jit(solution)/shard_map/psum | solution.py:97
  411.0 15.2 %slice-start.1 = ((s8[4718592]{0:T(1024)(128)(4,1)}), s8[4194304]{0:T(1024)(128)(4,1)S(1)}, s32[]{:S(2)}) async-start(s8[4718592]{0:T(1024)(128)(4,1)} %bitcast.66), calls=%async_computation.8 | async-start | bytes 8388608
  438.2 217.0 %reduce-scatter.5.cloned.1.call-start = ((), (), s32[]{:S(2)}) async-start(), calls=%async_computation.6 | async-start | bytes 5898240 | tf_op jit(solution)/shard_map/reduce_scatter | solution.py:122
  598.0 117.6 %reduce-scatter.3.cloned.1.call-start = ((), (), s32[]{:S(2)}) async-start(), calls=%async_computation.5 | async-start | bytes 5898240 | tf_op jit(solution)/shard_map/reduce_scatter | solution.py:121
Sparse Core Ops, SparseCore 0:
  9.8 98.9 all-gather.21
  277.3 133.6 all-reduce.3
  438.3 136.0 all-reduce.5
  598.1 57.0 reduce-scatter.4
  658.7 56.8 reduce-scatter.2
